TPU v7x, 256 devices: a whole 4x4x8 slice. The times are simulated.
256 devices in a mesh: section: 32 (over x, z), expert: 8 (over y, core).
Axes of the slice: x: 4, y: 4, z: 8, core: 2. Of those that a mesh axis runs over, the one named last changes fastest.
Arguments:
- tokens: bfloat16 [2048, 4096], P('expert', 'section'), may hold values from -6 to 6
- routes: int32 [2048, 2], P('expert'), may hold values from 0 to 7, all different within a row; in each aligned block of 256 rows (0 to 255, 256 to 511, ...) at most 80 rows name the same one
- mix_weights: float32 [2048, 2], P('expert'), may hold values from 0.2 to 1
- w_gate: bfloat16 [8, 4096, 8192], P('expert', None, 'section'), may hold values from -0.1875 to 0.1875
- w_up: bfloat16 [8, 4096, 8192], P('expert', None, 'section'), may hold values from -0.1875 to 0.1875
- w_down: bfloat16 [8, 8192, 4096], P('expert', 'section'), may hold values from -0.125 to 0.125
- upstream: bfloat16 [2048, 4096], P('expert', 'section'), may hold values from -6 to 6
Outputs:
- mixed: bfloat16 [2048, 4096], P('expert', 'section')
- grad_tokens: bfloat16 [2048, 4096], P('expert', 'section')
- grad_mix: float32 [2048, 2], P('expert')
- grad_gate: bfloat16 [8, 4096, 8192], P('expert', None, 'section')
- grad_up: bfloat16 [8, 4096, 8192], P('expert', None, 'section')
- grad_down: bfloat16 [8, 8192, 4096], P('expert', 'section')
Inputs may be any that keep to these rules, and one draw needn't show every extreme that they name: `routes`: each token names 2 different experts. Among the 256 tokens of one index of the expert axis no expert is named more than 80 times, and in some such block one expert is named exactly 80 times.
All inputs are finite; a program needn't handle non-finite values.
Results may differ from a plain program's by a relative error of at most 0.02.
Values may be sent and summed in bfloat16 or wider, within the bound.
No kernel may reach another device: no remote copies, remote signals or barrier semaphores. Data moves between devices by JAX's collectives and lax.ppermute only.
A program may use at most 128 MiB of HBM per device.

v0:
```python
import jax
import jax.numpy as jnp
from jax import lax
from jax.sharding import PartitionSpec as P

highest = lax.Precision.HIGHEST


def slot_tables(route_rows, mix_rows, capacity, experts):
    tok_count, top_count = route_rows.shape
    flat_routes = route_rows.reshape(-1)
    onehot = (flat_routes[:, None] == jnp.arange(experts, dtype=jnp.int32)[None, :]).astype(
        jnp.int32
    )
    earlier = jnp.cumsum(onehot, axis=0) - onehot
    position = jnp.sum(earlier * onehot, axis=1)
    target = (flat_routes * capacity + position).reshape(tok_count, top_count)
    slot_ids = jnp.arange(experts * capacity, dtype=jnp.int32)
    hits = target[None, :, :] == slot_ids[:, None, None]
    matches = hits.astype(jnp.float32)
    select = jnp.sum(matches, axis=2)
    weighted = jnp.sum(matches * mix_rows[None, :, :], axis=2)
    token_ids = jnp.arange(tok_count, dtype=jnp.int32)
    slot_token = jnp.sum(jnp.sum(hits.astype(jnp.int32), axis=2) * token_ids[None, :], axis=1)
    return (target, select, weighted, slot_token)


def per_device(tokens, routes, mix_weights, w_gate, w_up, w_down, upstream):
    experts = lax.axis_size("expert")
    tok_count = tokens.shape[0]
    top_count = routes.shape[1]
    capacity = 5 * tok_count * top_count // (4 * experts)
    slot_total = experts * capacity
    target, select, weighted, slot_token = slot_tables(routes, mix_weights, capacity, experts)
    slot_fill = jnp.sum(select, axis=1)
    slot_scale = jnp.sum(weighted, axis=1)
    gate_local = w_gate[0]
    up_local = w_up[0]
    down_local = w_down[0]

    def collect(source, factor):
        taken = source[slot_token].astype(jnp.float32)
        return (taken * factor[:, None]).astype(jnp.bfloat16)

    def to_experts(source, factor):
        block = collect(source, factor)
        arrived = lax.all_to_all(
            block.reshape(experts, capacity, -1), "expert", split_axis=0, concat_axis=0, tiled=True
        )
        whole = lax.all_gather(arrived, "section", axis=2, tiled=True)
        return whole.reshape(slot_total, -1)

    def to_sources(partial_value):
        summed = lax.psum_scatter(
            partial_value.reshape(experts, capacity, -1).astype(jnp.bfloat16),
            "section",
            scatter_dimension=2,
            tiled=True,
        )
        back = lax.all_to_all(summed, "expert", split_axis=0, concat_axis=0, tiled=True)
        return back.reshape(slot_total, -1)

    dispatched = to_experts(tokens, slot_fill)
    act_gate = jnp.dot(dispatched, gate_local, preferred_element_type=jnp.float32)
    act_up = jnp.dot(dispatched, up_local, preferred_element_type=jnp.float32)
    sig = jax.nn.sigmoid(act_gate)
    silu_gate = act_gate * sig
    hidden = (silu_gate * act_up).astype(jnp.bfloat16)
    partial_value = jnp.dot(hidden, down_local, preferred_element_type=jnp.float32)
    returned = to_sources(partial_value).astype(jnp.float32)
    moe_out = jnp.dot(weighted.T, returned, precision=highest)
    mixed = (tokens.astype(jnp.float32) + moe_out).astype(jnp.bfloat16)
    picked = returned[target]
    upstream_wide = upstream.astype(jnp.float32)
    mix_terms = jnp.einsum("tkd,td->tk", picked, upstream_wide, precision=highest)
    grad_mix = lax.psum(mix_terms, "section")
    grad_rows = to_experts(upstream, slot_scale)
    grad_hidden = lax.dot_general(
        grad_rows, down_local, (((1,), (1,)), ((), ())), preferred_element_type=jnp.float32
    )
    grad_down = lax.dot_general(
        hidden, grad_rows, (((0,), (0,)), ((), ())), preferred_element_type=jnp.float32
    ).astype(jnp.bfloat16)
    dsilu = sig * (1.0 + act_gate * (1.0 - sig))
    grad_act_gate = (grad_hidden * act_up * dsilu).astype(jnp.bfloat16)
    grad_act_up = (grad_hidden * silu_gate).astype(jnp.bfloat16)
    grad_gate = lax.dot_general(
        dispatched, grad_act_gate, (((0,), (0,)), ((), ())), preferred_element_type=jnp.float32
    ).astype(jnp.bfloat16)
    grad_up = lax.dot_general(
        dispatched, grad_act_up, (((0,), (0,)), ((), ())), preferred_element_type=jnp.float32
    ).astype(jnp.bfloat16)
    first = lax.dot_general(
        grad_act_gate, gate_local, (((1,), (1,)), ((), ())), preferred_element_type=jnp.float32
    )
    second = lax.dot_general(
        grad_act_up, up_local, (((1,), (1,)), ((), ())), preferred_element_type=jnp.float32
    )
    back_rows = to_sources(first + second).astype(jnp.float32)
    grad_moe = jnp.dot(select.T, back_rows, precision=highest)
    grad_tokens = (upstream_wide + grad_moe).astype(jnp.bfloat16)
    return (mixed, grad_tokens, grad_mix, grad_gate[None], grad_up[None], grad_down[None])


def solution(mesh):
    return jax.shard_map(
        per_device,
        mesh=mesh,
        in_specs=(
            P("expert", "section"),
            P("expert", None),
            P("expert", None),
            P("expert", None, "section"),
            P("expert", None, "section"),
            P("expert", "section", None),
            P("expert", "section"),
        ),
        out_specs=(
            P("expert", "section"),
            P("expert", "section"),
            P("expert", None),
            P("expert", None, "section"),
            P("expert", None, "section"),
            P("expert", "section", None),
        ),
        check_vma=False,
    )
```

profile of v0, /device:TPU:8, one launch (start us, length us, event | category | flops | bytes accessed | tf_op | source)
XLA Modules:
  0.0 783.5 jit_solution(15971595313948356913)
XLA Ops:
  11.4 2.1 select_reduce_fusion
  15.7 10.3 %all_to_all.20 = bf16[8,80,128]{2,1,0:T(8,128)(2,1)} all-to-all(bf16[8,80,128]{2,1,0:T(8,128)(2,1)S(1)} %fusion.17), channel_id=1, replica_groups=mesh['section'=32,'expert'=8] {'expert'}, dimensions={0} | all-to-all | bytes 327680 | tf_op jit(solution)/shard_map/all_to_all | solution.py:47
  28.3 9.5 %all_to_all.21 = bf16[8,80,128]{2,1,0:T(8,128)(2,1)} all-to-all(bf16[8,80,128]{2,1,0:T(8,128)(2,1)S(1)} %fusion.16), channel_id=1, replica_groups=mesh['section'=32,'expert'=8] {'expert'}, dimensions={0} | all-to-all | bytes 327680 | tf_op jit(solution)/shard_map/all_to_all | solution.py:47
  37.9 77.2 %all-gather.3.cloned.1.call-done = bf16[8,80,4096]{2,1,0:T(8,128)(2,1)} async-done(((bf16[8,80,128]{2,1,0:T(8,128)(2,1)}), bf16[8,80,4096]{2,1,0:T(8,128)(2,1)}) %all-gather.3.cloned.1.call-update) | async-done | bytes 5242896 | tf_op jit(solution)/shard_map/all_gather | solution.py:50
  115.2 5.7 fusion.7
  120.8 2.4 fusion.11
  123.2 81.6 %all-gather.5.cloned.1.call-done = bf16[8,80,4096]{2,1,0:T(8,128)(2,1)} async-done(((bf16[8,80,128]{2,1,0:T(8,128)(2,1)}), bf16[8,80,4096]{2,1,0:T(8,128)(2,1)}) %all-gather.5.cloned.1.call-update) | async-done | bytes 5242896 | tf_op jit(solution)/shard_map/all_gather | solution.py:50
  204.7 5.4 multiply_convert_fusion
  210.1 3.9 convolution_convert_fusion
  214.0 11.2 %copy.36 = bf16[8,80,4096]{1,0,2:T(8,128)(2,1)} copy(bf16[8,80,4096]{2,1,0:T(8,128)(2,1)} %convolution_convert_fusion) | data formatting | bytes 10485760
  225.2 13.1 %reshape.124 = bf16[4096,640]{1,0:T(8,128)(2,1)} reshape(bf16[4096,8,80]{2,1,0:T(8,128)(2,1)} %bitcast.66) | data formatting | bytes 10485760
  239.8 2.7 fusion.9
  242.5 3.9 add_convert_fusion
  246.4 11.2 %copy.38 = bf16[8,80,4096]{1,0,2:T(8,128)(2,1)} copy(bf16[8,80,4096]{2,1,0:T(8,128)(2,1)} %bitcast.69) | data formatting | bytes 10485760
  257.6 13.1 %reshape.126 = bf16[4096,640]{1,0:T(8,128)(2,1)} reshape(bf16[4096,8,80]{2,1,0:T(8,128)(2,1)} %bitcast.67) | data formatting | bytes 10485760
  271.7 5.7 fusion.1
  277.4 5.8 fusion
  283.2 180.6 %reduce-scatter.7.cloned.1.call-done = bf16[128,640]{1,0:T(8,128)(2,1)} async-done(((bf16[4096,640]{1,0:T(8,128)(2,1)}), bf16[128,640]{1,0:T(8,128)(2,1)}) %reduce-scatter.7.cloned.1.call-update) | async-done | bytes 163856
  465.8 4.8 all-to-all-start.1
  470.6 5.8 fusion.2
  476.4 215.3 %reduce-scatter.9.cloned.1.call-done = bf16[128,640]{1,0:T(8,128)(2,1)} async-done(((bf16[4096,640]{1,0:T(8,128)(2,1)}), bf16[128,640]{1,0:T(8,128)(2,1)}) %reduce-scatter.9.cloned.1.call-update) | async-done | bytes 163856
  693.7 4.8 all-to-all-start.3
  700.3 72.8 %psum.7 = f32[256,2]{0,1:T(2,128)} all-reduce(f32[256,2]{0,1:T(2,128)S(1)} %bitcast.81), channel_id=1, replica_groups=mesh['section'=32,'expert'=8] {'section'}, use_global_device_ids=true, to_apply=%region_11.12 | all-reduce | flops 512 | bytes 4096 | tf_op jit(solution)/shard_map/psum | solution.py:76
  773.2 2.4 fusion.13
  (65 shorter events, 18.5 us)
Async XLA Ops:
  7.2 197.6 %copy-start = (bf16[1,256,4096]{2,1,0:T(8,128)(2,1)S(1)}, bf16[1,256,4096]{2,1,0:T(8,128)(2,1)}, u32[]{:S(2)}) copy-start(bf16[1,256,4096]{2,1,0:T(8,128)(2,1)} %param.12) | copy-start | bytes 6291460
  7.2 6.4 copy-start.2
  7.2 18.9 %copy-start.3 = (bf16[256,128]{1,0:T(8,128)(2,1)S(1)}, bf16[256,128]{1,0:T(8,128)(2,1)}, u32[]{:S(2)}) copy-start(bf16[256,128]{1,0:T(8,128)(2,1)} %param.13) | copy-start | bytes 196612
  7.2 108.0 %all-gather.3.cloned.1.call-start = ((), (), s32[]{:S(2)}) async-start(), calls=%async_computation.6 | async-start | bytes 5406720 | tf_op jit(solution)/shard_map/all_gather | solution.py:50
  26.0 178.7 %all-gather.5.cloned.1.call-start = ((), (), s32[]{:S(2)}) async-start(), calls=%async_computation.7 | async-start | bytes 5406720 | tf_op jit(solution)/shard_map/all_gather | solution.py:50
  37.9 425.9 %reduce-scatter.7.cloned.1.call-start = ((), (), s32[]{:S(2)}) async-start(), calls=%async_computation.8 | async-start | bytes 5406720
  115.2 5.7 copy-start.4
  115.2 5.7 copy-start.10
  238.2 1.6 copy-start.5
  238.3 453.4 %reduce-scatter.9.cloned.1.call-start = ((), (), s32[]{:S(2)}) async-start(), calls=%async_computation.9 | async-start | bytes 5406720
  239.8 2.7 copy-start.6
  239.8 2.7 copy-start.8
  270.7 1.0 copy-start.9
  271.7 5.7 copy-start.7
  465.8 227.9 %all-to-all-start.1 = ((bf16[8,80,128]{2,1,0:T(8,128)(2,1)}), bf16[8,80,128]{2,1,0:T(8,128)(2,1)S(1)}, u32[]{:S(2)}, u32[]{:S(2)}) async-start(bf16[8,80,128]{2,1,0:T(8,128)(2,1)} %copy.37), calls=%async_computation.1 | async-start | bytes 327680 | tf_op jit(solution)/shard_map/all_to_all | solution.py:60
  470.6 306.3 %copy-start.1 = (bf16[1,256,4096]{2,1,0:T(8,128)(2,1)S(1)}, bf16[1,256,4096]{2,1,0:T(8,128)(2,1)}, u32[]{:S(2)}) copy-start(bf16[1,256,4096]{2,1,0:T(8,128)(2,1)} %param.12) | copy-start | bytes 6291460
  693.7 81.9 %all-to-all-start.3 = ((bf16[8,80,128]{2,1,0:T(8,128)(2,1)}), bf16[8,80,128]{2,1,0:T(8,128)(2,1)S(1)}, u32[]{:S(2)}, u32[]{:S(2)}) async-start(bf16[8,80,128]{2,1,0:T(8,128)(2,1)} %copy.39), calls=%async_computation.3 | async-start | bytes 327680 | tf_op jit(solution)/shard_map/all_to_all | solution.py:60
Sparse Core Ops, SparseCore 0:
  26.1 88.9 all-gather.2
  117.6 87.0 all-gather.4
  238.4 225.3 reduce-scatter.6
  467.6 224.0 reduce-scatter.8
where the time goes:
time: 785 us; the launch traced here: 783 us
  waiting for transfers between devices  555 us (71%)
  blocking collectives  92.6 us (12%)
  local copies, waits for them, and re-layouts  62.1 us (8%)
  matrix products  45.3 us (6%)
  between operations  14 us (2%)
  starting transfers between devices  9.93 us (1%)
    unnamed x6, waiting for transfers between devices  396 us
    all_gather x2, waiting for transfers between devices, to_experts(): whole = lax.all_gather(arrived, 'section', axis=2, tiled=True)  159 us
    psum x1, blocking collectives, per_device(): grad_mix = lax.psum(mix_terms, 'section')  72.8 us
    unnamed x31, local copies, waits for them, and re-layouts  55.6 us
    all_to_all x2, blocking collectives, to_experts(): lax.all_to_all(block.reshape(experts, capacity, -1), 'expert', split_axis...  19.8 us
  transfers between devices with their start and end apart: 6, of which 4 were waited for; matrix products, arithmetic and copies ran while one was open for 9% of the time, Pallas kernels for 0%

commit v1 on v0

--- a/solution.py
+++ b/solution.py
@@ -73,7 +73,7 @@
     picked = returned[target]
     upstream_wide = upstream.astype(jnp.float32)
     mix_terms = jnp.einsum("tkd,td->tk", picked, upstream_wide, precision=highest)
-    grad_mix = lax.psum(mix_terms, "section")
+    grad_mix = jnp.sum(lax.all_gather(mix_terms, "section"), axis=0)
     grad_rows = to_experts(upstream, slot_scale)
     grad_hidden = lax.dot_general(
         grad_rows, down_local, (((1,), (1,)), ((), ())), preferred_element_type=jnp.float32

time: 785 us -> 760 us (0.968)
  blocking collectives: 92.6 us -> 67.1 us
    psum x1 -> x0, blocking collectives: 72.8 us -> none  [per_device(): grad_mix = lax.psum(mix_terms, 'section')]
    all_gather x0 -> x1, blocking collectives: none -> 47.3 us  [per_device(): grad_mix = jnp.sum(lax.all_gather(mix_terms, 'section'), axis=0)]
where the time goes in v1:
time: 760 us; the launch traced here: 759 us
  waiting for transfers between devices  555 us (73%)
  blocking collectives  67.1 us (9%)
  local copies, waits for them, and re-layouts  62.1 us (8%)
  matrix products  45.3 us (6%)
  between operations  14 us (2%)
  starting transfers between devices  9.93 us (1%)
    unnamed x6, waiting for transfers between devices  396 us
    all_gather x2, waiting for transfers between devices, to_experts(): whole = lax.all_gather(arrived, 'section', axis=2, tiled=True)  159 us
    unnamed x31, local copies, waits for them, and re-layouts  55.6 us
    all_gather x1, blocking collectives, per_device(): grad_mix = jnp.sum(lax.all_gather(mix_terms, 'section'), axis=0)  47.3 us
    all_to_all x2, blocking collectives, to_experts(): lax.all_to_all(block.reshape(experts, capacity, -1), 'expert', split_axis...  19.8 us
  transfers between devices with their start and end apart: 6, of which 4 were waited for; matrix products, arithmetic and copies ran while one was open for 9% of the time, Pallas kernels for 0%

profile of v1, /device:TPU:8, one launch (start us, length us, event | category | flops | bytes accessed | tf_op | source)
XLA Modules:
  0.0 758.6 jit_solution(1219701006965071149)
XLA Ops:
  11.4 2.1 select_reduce_fusion
  15.7 10.3 %all_to_all.20 = bf16[8,80,128]{2,1,0:T(8,128)(2,1)} all-to-all(bf16[8,80,128]{2,1,0:T(8,128)(2,1)S(1)} %fusion.17), channel_id=1, replica_groups=mesh['section'=32,'expert'=8] {'expert'}, dimensions={0} | all-to-all | bytes 327680 | tf_op jit(solution)/shard_map/all_to_all | solution.py:47
  28.3 9.5 %all_to_all.21 = bf16[8,80,128]{2,1,0:T(8,128)(2,1)} all-to-all(bf16[8,80,128]{2,1,0:T(8,128)(2,1)S(1)} %fusion.16), channel_id=1, replica_groups=mesh['section'=32,'expert'=8] {'expert'}, dimensions={0} | all-to-all | bytes 327680 | tf_op jit(solution)/shard_map/all_to_all | solution.py:47
  37.9 77.2 %all-gather.4.cloned.1.call-done = bf16[8,80,4096]{2,1,0:T(8,128)(2,1)} async-done(((bf16[8,80,128]{2,1,0:T(8,128)(2,1)}), bf16[8,80,4096]{2,1,0:T(8,128)(2,1)}) %all-gather.4.cloned.1.call-update) | async-done | bytes 5242896 | tf_op jit(solution)/shard_map/all_gather | solution.py:50
  115.2 5.7 fusion.7
  120.8 2.4 fusion.11
  123.2 81.6 %all-gather.6.cloned.1.call-done = bf16[8,80,4096]{2,1,0:T(8,128)(2,1)} async-done(((bf16[8,80,128]{2,1,0:T(8,128)(2,1)}), bf16[8,80,4096]{2,1,0:T(8,128)(2,1)}) %all-gather.6.cloned.1.call-update) | async-done | bytes 5242896 | tf_op jit(solution)/shard_map/all_gather | solution.py:50
  204.7 5.4 multiply_convert_fusion
  210.1 3.9 convolution_convert_fusion
  214.0 11.2 %copy.36 = bf16[8,80,4096]{1,0,2:T(8,128)(2,1)} copy(bf16[8,80,4096]{2,1,0:T(8,128)(2,1)} %convolution_convert_fusion) | data formatting | bytes 10485760
  225.2 13.1 %reshape.125 = bf16[4096,640]{1,0:T(8,128)(2,1)} reshape(bf16[4096,8,80]{2,1,0:T(8,128)(2,1)} %bitcast.71) | data formatting | bytes 10485760
  239.8 2.7 fusion.9
  242.5 3.9 add_convert_fusion
  246.4 11.2 %copy.38 = bf16[8,80,4096]{1,0,2:T(8,128)(2,1)} copy(bf16[8,80,4096]{2,1,0:T(8,128)(2,1)} %bitcast.74) | data formatting | bytes 10485760
  257.6 13.1 %reshape.127 = bf16[4096,640]{1,0:T(8,128)(2,1)} reshape(bf16[4096,8,80]{2,1,0:T(8,128)(2,1)} %bitcast.72) | data formatting | bytes 10485760
  271.7 5.7 fusion.1
  277.4 5.8 fusion
  283.2 180.6 %reduce-scatter.7.cloned.1.call-done = bf16[128,640]{1,0:T(8,128)(2,1)} async-done(((bf16[4096,640]{1,0:T(8,128)(2,1)}), bf16[128,640]{1,0:T(8,128)(2,1)}) %reduce-scatter.7.cloned.1.call-update) | async-done | bytes 163856
  465.8 4.8 all-to-all-start.1
  470.6 5.8 fusion.2
  476.4 215.3 %reduce-scatter.9.cloned.1.call-done = bf16[128,640]{1,0:T(8,128)(2,1)} async-done(((bf16[4096,640]{1,0:T(8,128)(2,1)}), bf16[128,640]{1,0:T(8,128)(2,1)}) %reduce-scatter.9.cloned.1.call-update) | async-done | bytes 163856
  693.7 4.8 all-to-all-start.3
  698.5 2.4 fusion.13
  702.8 47.3 %all-gather = f32[8192,2]{0,1:T(2,128)S(1)} all-gather(f32[256,2]{0,1:T(2,128)S(1)} %bitcast.87), channel_id=2, replica_groups=mesh['section'=32,'expert'=8] {'section'}, dimensions={0}, use_global_device_ids=true | all-gather | bytes 67584 | tf_op jit(solution)/shard_map/all_gather | solution.py:76
  (66 shorter events, 19.1 us)
Async XLA Ops:
  7.2 197.6 %copy-start = (bf16[1,256,4096]{2,1,0:T(8,128)(2,1)S(1)}, bf16[1,256,4096]{2,1,0:T(8,128)(2,1)}, u32[]{:S(2)}) copy-start(bf16[1,256,4096]{2,1,0:T(8,128)(2,1)} %param.12) | copy-start | bytes 6291460
  7.2 6.4 copy-start.2
  7.2 18.9 %copy-start.3 = (bf16[256,128]{1,0:T(8,128)(2,1)S(1)}, bf16[256,128]{1,0:T(8,128)(2,1)}, u32[]{:S(2)}) copy-start(bf16[256,128]{1,0:T(8,128)(2,1)} %param.13) | copy-start | bytes 196612
  7.2 108.0 %all-gather.4.cloned.1.call-start = ((), (), s32[]{:S(2)}) async-start(), calls=%async_computation.6 | async-start | bytes 5406720 | tf_op jit(solution)/shard_map/all_gather | solution.py:50
  26.0 178.7 %all-gather.6.cloned.1.call-start = ((), (), s32[]{:S(2)}) async-start(), calls=%async_computation.7 | async-start | bytes 5406720 | tf_op jit(solution)/shard_map/all_gather | solution.py:50
  37.9 425.9 %reduce-scatter.7.cloned.1.call-start = ((), (), s32[]{:S(2)}) async-start(), calls=%async_computation.8 | async-start | bytes 5406720
  115.2 5.7 copy-start.4
  115.2 5.7 copy-start.10
  238.2 1.6 copy-start.5
  238.3 453.4 %reduce-scatter.9.cloned.1.call-start = ((), (), s32[]{:S(2)}) async-start(), calls=%async_computation.9 | async-start | bytes 5406720
  239.8 2.7 copy-start.6
  239.8 2.7 copy-start.8
  270.7 1.0 copy-start.9
  271.7 5.7 copy-start.7
  465.8 227.9 %all-to-all-start.1 = ((bf16[8,80,128]{2,1,0:T(8,128)(2,1)}), bf16[8,80,128]{2,1,0:T(8,128)(2,1)S(1)}, u32[]{:S(2)}, u32[]{:S(2)}) async-start(bf16[8,80,128]{2,1,0:T(8,128)(2,1)} %copy.37), calls=%async_computation.1 | async-start | bytes 327680 | tf_op jit(solution)/shard_map/all_to_all | solution.py:60
  470.6 281.4 %copy-start.1 = (bf16[1,256,4096]{2,1,0:T(8,128)(2,1)S(1)}, bf16[1,256,4096]{2,1,0:T(8,128)(2,1)}, u32[]{:S(2)}) copy-start(bf16[1,256,4096]{2,1,0:T(8,128)(2,1)} %param.12) | copy-start | bytes 6291460
  693.7 57.0 %all-to-all-start.3 = ((bf16[8,80,128]{2,1,0:T(8,128)(2,1)}), bf16[8,80,128]{2,1,0:T(8,128)(2,1)S(1)}, u32[]{:S(2)}, u32[]{:S(2)}) async-start(bf16[8,80,128]{2,1,0:T(8,128)(2,1)} %copy.39), calls=%async_computation.3 | async-start | bytes 327680 | tf_op jit(solution)/shard_map/all_to_all | solution.py:60
Sparse Core Ops, SparseCore 0:
  26.1 88.9 all-gather.3
  117.6 87.0 all-gather.5
  238.4 225.3 reduce-scatter.6
  467.6 224.0 reduce-scatter.8
